TPU v7x, 512 devices: a whole 4x4x16 slice. The times are simulated.
512 devices in a mesh: aux: 128 (over x, z, core), occ: 4 (over y).
Axes of the slice: x: 4, y: 4, z: 16, core: 2. Of those that a mesh axis runs over, the one named last changes fastest.
Arguments:
- half_ints: bfloat16 [8192, 3, 2560], P('aux', None, 'occ'), may hold values from -1.75 to 1.75
- coef_virt: bfloat16 [2048, 2560], P('aux', 'occ'), may hold values from -0.125 to 0.125
- screen: int32 [256, 20], P('aux', 'occ'), may hold values from 0 to 1, as said below
- occ_energy: float32 [512], replicated, may hold values from -2 to -0.3
- virt_energy: float32 [2048], replicated, may hold values from 0.2 to 4
- batch_orbitals: int32 [3], replicated, may hold values from 0 to 511, as said below
Outputs:
- amplitudes: float32 [128, 3, 256, 3, 128], P('aux', None, 'occ')
- gamma: bfloat16 [8192, 3, 2048], P(('aux', 'occ'))
Inputs may be any that keep to these rules, and one draw needn't show every extreme that they name: `screen`: 1 where a block of 32 auxiliary and 128 atomic functions is kept, 0 where it is screened out. `batch_orbitals`: 3 distinct occupied orbitals, among them the first and the last.
All inputs are finite; a program needn't handle non-finite values.
Results may differ from a plain program's by a relative error of at most 0.006.
Values may be sent and summed in bfloat16 or wider, within the bound.
No kernel may reach another device: no remote copies, remote signals or barrier semaphores. Data moves between devices by JAX's collectives and lax.ppermute only.
A program may use at most 64 MiB of HBM per device.

v0:
```python
import jax
import jax.numpy as jnp
from jax import lax
from jax.sharding import Mesh
from jax.sharding import PartitionSpec as P

BF = jnp.bfloat16
F32 = jnp.float32


def swap_cores(value):
    return lax.ppermute(value, "c", [(0, 1), (1, 0)])


def exchange(value, axis):
    members, rows, lanes = value.shape
    value = value.reshape(members * rows, lanes)
    value = lax.all_to_all(value, axis, split_axis=0, concat_axis=0, tiled=True)
    return value.reshape(members, rows, lanes)


def by_core(mine, theirs, core):
    return (jnp.where(core == 0, mine, theirs), jnp.where(core == 0, theirs, mine))


def local(half_ints, coef_virt, screen, occ_energy, virt_energy, batch_orbitals):
    p_rows, nocc, ao_part = half_ints.shape
    nv = virt_energy.shape[0]
    nx, nz, ny = (lax.axis_size("x"), lax.axis_size("z"), lax.axis_size("y"))
    nl = nz // 2
    x, z, c, y = (lax.axis_index(name) for name in ("x", "z", "c", "y"))
    zh, zl = (z // nl, z % nl)
    r = p_rows // ny
    wide = nv // nx
    narrow = nv // nz
    half = wide // 2
    share = half // ny
    ways = wide // narrow
    labels = jnp.arange(occ_energy.shape[0], dtype=jnp.int32)
    onehot = (batch_orbitals[:, None] == labels[None, :]).astype(F32)
    slot_energy = jnp.sum(onehot * occ_energy[None, :], axis=1)
    with jax.named_scope("transform"):
        copies = jnp.broadcast_to(coef_virt[None], (nz,) + coef_virt.shape)
        coef = exchange(copies, "z")
        expanded = jnp.repeat(jnp.repeat(screen, 32, axis=0), 128, axis=1).astype(BF)
        masked = half_ints * expanded[:, None, :]
        masked = masked.reshape(ny, r, nocc, ao_part).transpose(0, 2, 1, 3)
        masked = lax.all_gather(masked.reshape(-1, ao_part), "x", axis=0)
        masked = masked.reshape(nx, ny, nocc, r, ao_part)
        masked, coef = lax.optimization_barrier((masked, coef))
        low, high = by_core(coef, swap_cores(coef), c)
        coef = jnp.stack([low, high], axis=1).reshape(wide, ao_part)
        part = jnp.einsum("xyirm,am->yxira", masked, coef, preferred_element_type=F32)
        part = exchange(part.astype(BF).reshape(ny, nx * nocc * r, wide), "y")
        three = jnp.sum(part.astype(F32), axis=0).astype(BF).reshape(nx, nocc, r, wide)
    with jax.named_scope("panels"):
        row = jnp.concatenate([three[:, i] for i in range(nocc)], axis=-1)
        row = lax.all_gather(row.reshape(nx * r, nocc * wide), "z", axis=0, tiled=True)
        col = exchange(three.reshape(nx, nocc * r, wide), "x")
        col = col.reshape(nx, nocc, r, ways // 2, 2, narrow)
        col = jnp.concatenate(
            [col[:, i].transpose(3, 0, 2, 1, 4).reshape(nz, r, narrow) for i in range(nocc)],
            axis=-1,
        )
        col = exchange(col, "z")
        col = lax.all_gather(col.reshape(nz * r, nocc * narrow), "x", axis=0)
        col = col.reshape(nx, nz, r, nocc * narrow)
        col = col.transpose(1, 0, 2, 3).reshape(nz * nx * r, nocc * narrow)
    with jax.named_scope("gram"):
        gram = lax.dot_general(row, col, (((0,), (0,)), ((), ())), preferred_element_type=F32)
        gram = gram.reshape(nocc, 2, half, nocc * narrow)
        mine = lax.dynamic_index_in_dim(gram, c, 1, keepdims=False)
        other = lax.dynamic_index_in_dim(gram, 1 - c, 1, keepdims=False)
        gram = mine + swap_cores(other)
        gram = gram.reshape(nocc, ny, share, nocc * narrow).transpose(1, 0, 2, 3)
        gram = exchange(gram.astype(BF).reshape(ny, nocc * share, nocc * narrow), "y")
        gram = jnp.sum(gram.astype(F32), axis=0).reshape(nocc, share, nocc, narrow)
    with jax.named_scope("amplitudes"):
        row_energy = lax.dynamic_slice_in_dim(
            virt_energy, x * wide + c * half + y * share, share, 0
        )
        col_energy = lax.dynamic_slice_in_dim(virt_energy, (zl * 2 + zh) * narrow, narrow, 0)
        denominators = (
            slot_energy[:, None, None, None]
            + slot_energy[None, None, :, None]
            - row_energy[None, :, None, None]
            - col_energy[None, None, None, :]
        )
        amps = gram / denominators
        mixed = (2.0 * amps - jnp.transpose(amps, (2, 1, 0, 3))).astype(BF)
        swap = []
        for h in range(2):
            for l in range(nl):
                for k in range(2):
                    swap.append(((h * nl + l) * 2 + k, (k * nl + l) * 2 + h))
        own = lax.ppermute(amps, ("z", "c"), swap)
        mixed = jnp.concatenate([mixed[:, :, j] for j in range(nocc)], axis=-1)
        mixed = lax.all_gather(mixed.reshape(nocc * share, nocc * narrow), "y", axis=0)
        mixed = mixed.reshape(ny, nocc, share, nocc * narrow).transpose(1, 0, 2, 3)
        mixed = mixed.reshape(nocc, half, nocc * narrow)
        low, high = by_core(mixed, swap_cores(mixed), c)
        mixed = jnp.stack([low, high], axis=1).reshape(nocc * wide, nocc * narrow)
    with jax.named_scope("gamma"):
        value = jnp.dot(row, mixed, preferred_element_type=F32).astype(BF)
        value = value.reshape(nz, nx, r, nocc * narrow).transpose(1, 0, 2, 3)
        value = exchange(value.reshape(nx, nz * r, nocc * narrow), "x")
        value = jnp.sum(value.astype(F32), axis=0).astype(BF)
        value = exchange(value.reshape(nz, r, nocc * narrow), "z")
        value = value.reshape(2, nl, r, nocc, narrow).transpose(2, 3, 1, 0, 4)
        gamma = value.reshape(r, nocc, nv)
    return (own[None], gamma)


def solution(mesh):
    fine = Mesh(
        mesh.devices.reshape(4, mesh.shape["aux"] // 8, 2, mesh.shape["occ"]), ("x", "z", "c", "y")
    )
    aux = ("x", "z", "c")
    in_specs = (P(aux, None, "y"), P(aux, "y"), P(aux, "y"), P(), P(), P())
    out_specs = (P(aux, None, "y", None, None), P(aux + ("y",), None, None))
    return jax.shard_map(local, mesh=fine, in_specs=in_specs, out_specs=out_specs, check_vma=False)
```

profile of v0, /device:TPU:1, one launch (start us, length us, event | category | flops | bytes accessed | tf_op | source)
XLA Modules:
  0.0 264.1 jit_solution(2619876952096611985)
XLA Ops:
  7.2 1.5 broadcast_in_dim.10
  8.7 15.7 %all-to-all-start = ((bf16[16,16,640]{2,1,0:T(8,128)(2,1)}), bf16[16,16,640]{2,1,0:T(8,128)(2,1)S(1)}, u32[]{:S(2)}, u32[]{:S(2)}) async-start(bf16[16,16,640]{2,1,0:T(8,128)(2,1)} %broadcast_in_dim.10), calls=%async_computation | async-start | bytes 655360 | tf_op jit(solution)/shard_map/transform/all_to_all | solution.py:18
  24.5 0.7 convert_element_type.44
  25.4 13.2 %all_gather.12 = bf16[4,192,640]{2,1,0:T(8,128)(2,1)S(1)} all-gather(bf16[1,192,640]{2,1,0:T(8,128)(2,1)S(1)} %bitcast.110), channel_id=1, replica_groups=mesh['x'=4,'z'=16,'c'=2,'y'=4] {'x'}, dimensions={0}, use_global_device_ids=true | all-gather | bytes 1228800 | tf_op jit(solution)/shard_map/transform/all_gather | solution.py:48
  38.7 1.0 all-to-all-done
  39.7 8.4 %collective-permute-start = (bf16[16,16,640]{2,1,0:T(8,128)(2,1)S(1)}, bf16[16,16,640]{2,1,0:T(8,128)(2,1)S(1)}, u32[]{:S(2)}, u32[]{:S(2)}) collective-permute-start(bf16[16,16,640]{2,1,0:T(8,128)(2,1)S(1)} %all-to-all-done), channel_id=1, source_target_pairs={{0,4},{4,0},{1,5},{5,1},{2,6},{6,2},{3,7},{7,3},{8,12},{12,8},{9,1... | collective-permute-start | bytes 983048 | tf_op jit(solution)/shard_map/transform/ppermute | solution.py:12
  48.1 1.2 collective-permute-done
  49.5 0.8 fusion
  50.3 15.4 %all_to_all.57 = bf16[4,192,512]{2,1,0:T(8,128)(2,1)S(1)} all-to-all(bf16[4,192,512]{2,1,0:T(8,128)(2,1)S(1)} %bitcast.100), channel_id=1, replica_groups=mesh['x'=4,'z'=16,'c'=2,'y'=4] {'y'}, dimensions={0} | all-to-all | bytes 1572864 | tf_op jit(solution)/shard_map/transform/all_to_all | solution.py:18
  65.7 0.1 reduce_sum.42
  65.9 0.7 pad_maximum_fusion.2
  66.6 9.0 %all_to_all.58 = bf16[4,48,512]{2,1,0:T(8,128)(2,1)S(1)} all-to-all(bf16[4,48,512]{2,1,0:T(8,128)(2,1)S(1)} %bitcast.107), channel_id=1, replica_groups=mesh['x'=4,'z'=16,'c'=2,'y'=4] {'x'}, dimensions={0} | all-to-all | bytes 393216 | tf_op jit(solution)/shard_map/panels/all_to_all | solution.py:18
  75.7 0.2 slice_bitcast_fusion.2
  75.9 0.7 pad_maximum_fusion.3
  76.6 6.7 %all-to-all-start.3 = ((bf16[16,16,384]{2,1,0:T(8,128)(2,1)}), bf16[16,16,384]{2,1,0:T(8,128)(2,1)S(1)}, u32[]{:S(2)}, u32[]{:S(2)}) async-start(bf16[16,16,384]{2,1,0:T(8,128)(2,1)} %pad_maximum_fusion.3), calls=%async_computation.3 | async-start | bytes 393216 | tf_op jit(solution)/shard_map/panels/all_to_all | solution.py:18
  83.3 15.0 %all-to-all-done.3 = bf16[16,16,384]{2,1,0:T(8,128)(2,1)S(1)} async-done(((bf16[16,16,384]{2,1,0:T(8,128)(2,1)}), bf16[16,16,384]{2,1,0:T(8,128)(2,1)S(1)}, u32[]{:S(2)}, u32[]{:S(2)}) %all-to-all-start.3) | async-done | bytes 196640 | tf_op jit(solution)/shard_map/panels/all_to_all | solution.py:18
  98.3 11.9 %all_gather.14 = bf16[4,256,384]{2,1,0:T(8,128)(2,1)S(1)} all-gather(bf16[1,256,384]{2,1,0:T(8,128)(2,1)S(1)} %bitcast.115), channel_id=1, replica_groups=mesh['x'=4,'z'=16,'c'=2,'y'=4] {'x'}, dimensions={0}, use_global_device_ids=true | all-gather | bytes 983040 | tf_op jit(solution)/shard_map/panels/all_gather | solution.py:66
  110.1 1.0 copy.61
  111.2 25.6 %all-gather.2.cloned.1.call-done = bf16[1024,1536]{1,0:T(8,128)(2,1)} async-done(((bf16[64,1536]{1,0:T(8,128)(2,1)}), bf16[1024,1536]{1,0:T(8,128)(2,1)}) %all-gather.2.cloned.1.call-update) | async-done | bytes 3145744 | tf_op jit(solution)/shard_map/panels/all_gather | solution.py:58
  136.7 3.2 %copy.57 = bf16[1536,1024]{1,0:T(8,128)(2,1)S(1)} copy(bf16[1536,1024]{0,1:T(8,128)(2,1)} %bitcast.98) | data formatting | bytes 6291456 | tf_op jit(solution)/shard_map/gram/dot_general | solution.py:70
  139.9 2.9 %fusion.5 = f32[3,2,256,384]{3,2,1,0:T(8,128)S(1)} fusion(bf16[3,2,256,1024]{3,2,1,0:T(8,128)(2,1)S(1)} %bitcast.99, bf16[1024,384,1,1]{1,0,3,2:T(8,128)(2,1)} %bitcast.113), kind=kOutput, calls=%fused_computation.31 | convolution fusion | flops 1207959552 | bytes 6291456 | tf_op jit(solution)/shard_map/gram/dot_general | solution.py:70
  143.0 1.3 copy-done.1
  144.3 10.6 %collective-permute-start.1 = (f32[3,256,384]{2,1,0:T(8,128)S(1)}, f32[3,256,384]{2,1,0:T(8,128)S(1)}, u32[]{:S(2)}, u32[]{:S(2)}) collective-permute-start(f32[3,256,384]{2,1,0:T(8,128)S(1)} %dynamic-slice_bitcast_fusion), channel_id=1, source_target_pairs={{0,4},{4,0},{1,5},{5,1},{2,6},{6,2},{3,7},{7,3},{8,12},{12,8},{9,1... | collective-permute-start | bytes 3538952 | tf_op jit(solution)/shard_map/gram/ppermute | solution.py:12
  154.9 0.8 dynamic_slice.16
  155.7 0.8 dynamic_slice.15
  156.5 0.2 select_reduce_fusion
  156.7 0.7 collective-permute-done.1
  157.4 1.4 fusion.1
  158.7 0.9 copy.62
  159.6 3.5 %all-to-all-start.4 = ((bf16[4,192,384]{2,1,0:T(8,128)(2,1)}), bf16[4,192,384]{2,1,0:T(8,128)(2,1)S(1)}, u32[]{:S(2)}, u32[]{:S(2)}) async-start(bf16[4,192,384]{2,1,0:T(8,128)(2,1)} %bitcast.39), calls=%async_computation.4 | async-start | bytes 1179648 | tf_op jit(solution)/shard_map/gram/all_to_all | solution.py:18
  163.3 9.5 %all-to-all-done.4 = bf16[4,192,384]{2,1,0:T(8,128)(2,1)S(1)} async-done(((bf16[4,192,384]{2,1,0:T(8,128)(2,1)}), bf16[4,192,384]{2,1,0:T(8,128)(2,1)S(1)}, u32[]{:S(2)}, u32[]{:S(2)}) %all-to-all-start.4) | async-done | bytes 589856 | tf_op jit(solution)/shard_map/gram/all_to_all | solution.py:18
  173.0 0.3 subtract_divide_fusion
  173.3 0.3 fusion.2
  173.7 11.0 %all_gather.15 = bf16[4,192,384]{2,1,0:T(8,128)(2,1)S(1)} all-gather(bf16[1,192,384]{2,1,0:T(8,128)(2,1)S(1)} %pad_maximum_fusion.4), channel_id=1, replica_groups=mesh['x'=4,'z'=16,'c'=2,'y'=4] {'y'}, dimensions={0}, use_global_device_ids=true | all-gather | bytes 737280 | tf_op jit(solution)/shard_map/amplitudes/all_gather | solution.py:98
  184.8 6.0 %collective-permute-start.3 = (bf16[3,256,384]{2,1,0:T(8,128)(2,1)S(1)}, bf16[3,256,384]{2,1,0:T(8,128)(2,1)S(1)}, u32[]{:S(2)}, u32[]{:S(2)}) collective-permute-start(bf16[3,256,384]{2,1,0:T(8,128)(2,1)S(1)} %bitcast.103), channel_id=1, source_target_pairs={{0,4},{4,0},{1,5},{5,1},{2,6},{6,2},{3,7},{7,3},{8,12},{12,8},{9,1... | collective-permute-start | bytes 1769480 | tf_op jit(solution)/shard_map/amplitudes/ppermute | solution.py:12
  190.8 1.6 collective-permute-done.3
  192.4 0.2 select_bitcast_fusion.1
  192.6 0.1 pad_maximum_fusion
  192.8 1.6 copy-done
  194.4 1.8 convolution_convert_fusion
  196.3 16.3 %all_to_all.59 = bf16[4,256,384]{2,1,0:T(8,128)(2,1)S(1)} all-to-all(bf16[4,256,384]{2,1,0:T(8,128)(2,1)S(1)} %bitcast.101), channel_id=1, replica_groups=mesh['x'=4,'z'=16,'c'=2,'y'=4] {'x'}, dimensions={0} | all-to-all | bytes 1572864 | tf_op jit(solution)/shard_map/gamma/all_to_all | solution.py:18
  212.6 0.8 reduce_sum.45
  213.4 6.5 %all-to-all-start.6 = ((bf16[16,16,384]{2,1,0:T(8,128)(2,1)}), bf16[16,16,384]{2,1,0:T(8,128)(2,1)S(1)}, u32[]{:S(2)}, u32[]{:S(2)}) async-start(bf16[16,16,384]{2,1,0:T(8,128)(2,1)} %bitcast.54), calls=%async_computation.6 | async-start | bytes 393216 | tf_op jit(solution)/shard_map/gamma/all_to_all | solution.py:18
  219.9 14.2 %collective-permute-start.2 = (f32[3,64,3,128]{3,2,1,0:T(4,128)S(1)}, f32[3,64,3,128]{3,2,1,0:T(4,128)S(1)}, u32[]{:S(2)}, u32[]{:S(2)}) collective-permute-start(f32[3,64,3,128]{3,2,1,0:T(4,128)S(1)} %subtract_divide_fusion), channel_id=1, source_target_pairs={{0,0},{4,64},{8,8},{12,72},{16,16},{20,80},{24,24},{28,88},{32,32}... | collective-permute-start | bytes 884744 | tf_op jit(solution)/shard_map/amplitudes/ppermute | solution.py:96
  234.2 21.2 %collective-permute-done.2 = f32[3,64,3,128]{3,2,1,0:T(4,128)S(1)} collective-permute-done((f32[3,64,3,128]{3,2,1,0:T(4,128)S(1)}, f32[3,64,3,128]{3,2,1,0:T(4,128)S(1)}, u32[]{:S(2)}, u32[]{:S(2)}) %collective-permute-start.2) | collective-permute-done | bytes 294944 | tf_op jit(solution)/shard_map/amplitudes/ppermute | solution.py:96
  255.4 0.7 copy.71
  256.2 0.2 copy.70
  256.5 0.8 reshape.185
  (38 shorter events, 1.5 us)
Async XLA Ops:
  7.2 18.2 %copy-start.2 = (bf16[64,3,640]{2,0,1:T(8,128)(2,1)S(1)}, bf16[64,3,640]{2,0,1:T(8,128)(2,1)}, u32[]{:S(2)}) copy-start(bf16[64,3,640]{2,0,1:T(8,128)(2,1)} %param.6) | copy-start | bytes 737284
  8.7 31.0 %all-to-all-start = ((bf16[16,16,640]{2,1,0:T(8,128)(2,1)}), bf16[16,16,640]{2,1,0:T(8,128)(2,1)S(1)}, u32[]{:S(2)}, u32[]{:S(2)}) async-start(bf16[16,16,640]{2,1,0:T(8,128)(2,1)} %broadcast_in_dim.10), calls=%async_computation | async-start | bytes 655360 | tf_op jit(solution)/shard_map/transform/all_to_all | solution.py:18
  24.4 112.3 %all-gather.2.cloned.1.call-start = ((), (), s32[]{:S(2)}) async-start(), calls=%async_computation.7 | async-start | bytes 3342336 | tf_op jit(solution)/shard_map/panels/all_gather | solution.py:58
  39.7 9.6 %collective-permute-start = (bf16[16,16,640]{2,1,0:T(8,128)(2,1)S(1)}, bf16[16,16,640]{2,1,0:T(8,128)(2,1)S(1)}, u32[]{:S(2)}, u32[]{:S(2)}) collective-permute-start(bf16[16,16,640]{2,1,0:T(8,128)(2,1)S(1)} %all-to-all-done), channel_id=1, source_target_pairs={{0,4},{4,0},{1,5},{5,1},{2,6},{6,2},{3,7},{7,3},{8,12},{12,8},{9,1... | collective-permute-start | bytes 983048 | tf_op jit(solution)/shard_map/transform/ppermute | solution.py:12
  76.6 21.6 %all-to-all-start.3 = ((bf16[16,16,384]{2,1,0:T(8,128)(2,1)}), bf16[16,16,384]{2,1,0:T(8,128)(2,1)S(1)}, u32[]{:S(2)}, u32[]{:S(2)}) async-start(bf16[16,16,384]{2,1,0:T(8,128)(2,1)} %pad_maximum_fusion.3), calls=%async_computation.3 | async-start | bytes 393216 | tf_op jit(solution)/shard_map/panels/all_to_all | solution.py:18
  142.9 1.5 copy-start.1
  142.9 13.6 %copy-start.3 = (f32[512]{0:T(512)S(1)}, f32[512]{0:T(512)}, u32[]{:S(2)}) copy-start(f32[512]{0:T(512)} %param.9) | copy-start | bytes 6148
  142.9 13.6 %copy-start.4 = (s32[3]{0:T(128)S(1)}, s32[3]{0:T(128)}, u32[]{:S(2)}) copy-start(s32[3]{0:T(128)} %param.11) | copy-start | bytes 40
  144.3 13.0 %collective-permute-start.1 = (f32[3,256,384]{2,1,0:T(8,128)S(1)}, f32[3,256,384]{2,1,0:T(8,128)S(1)}, u32[]{:S(2)}, u32[]{:S(2)}) collective-permute-start(f32[3,256,384]{2,1,0:T(8,128)S(1)} %dynamic-slice_bitcast_fusion), channel_id=1, source_target_pairs={{0,4},{4,0},{1,5},{5,1},{2,6},{6,2},{3,7},{7,3},{8,12},{12,8},{9,1... | collective-permute-start | bytes 3538952 | tf_op jit(solution)/shard_map/gram/ppermute | solution.py:12
  159.6 13.2 %all-to-all-start.4 = ((bf16[4,192,384]{2,1,0:T(8,128)(2,1)}), bf16[4,192,384]{2,1,0:T(8,128)(2,1)S(1)}, u32[]{:S(2)}, u32[]{:S(2)}) async-start(bf16[4,192,384]{2,1,0:T(8,128)(2,1)} %bitcast.39), calls=%async_computation.4 | async-start | bytes 1179648 | tf_op jit(solution)/shard_map/gram/all_to_all | solution.py:18
  184.8 7.6 %collective-permute-start.3 = (bf16[3,256,384]{2,1,0:T(8,128)(2,1)S(1)}, bf16[3,256,384]{2,1,0:T(8,128)(2,1)S(1)}, u32[]{:S(2)}, u32[]{:S(2)}) collective-permute-start(bf16[3,256,384]{2,1,0:T(8,128)(2,1)S(1)} %bitcast.103), channel_id=1, source_target_pairs={{0,4},{4,0},{1,5},{5,1},{2,6},{6,2},{3,7},{7,3},{8,12},{12,8},{9,1... | collective-permute-start | bytes 1769480 | tf_op jit(solution)/shard_map/amplitudes/ppermute | solution.py:12
  192.5 1.9 copy-start
  213.4 42.7 %all-to-all-start.6 = ((bf16[16,16,384]{2,1,0:T(8,128)(2,1)}), bf16[16,16,384]{2,1,0:T(8,128)(2,1)S(1)}, u32[]{:S(2)}, u32[]{:S(2)}) async-start(bf16[16,16,384]{2,1,0:T(8,128)(2,1)} %bitcast.54), calls=%async_computation.6 | async-start | bytes 393216 | tf_op jit(solution)/shard_map/gamma/all_to_all | solution.py:18
  219.9 35.5 %collective-permute-start.2 = (f32[3,64,3,128]{3,2,1,0:T(4,128)S(1)}, f32[3,64,3,128]{3,2,1,0:T(4,128)S(1)}, u32[]{:S(2)}, u32[]{:S(2)}) collective-permute-start(f32[3,64,3,128]{3,2,1,0:T(4,128)S(1)} %subtract_divide_fusion), channel_id=1, source_target_pairs={{0,0},{4,64},{8,8},{12,72},{16,16},{20,80},{24,24},{28,88},{32,32}... | collective-permute-start | bytes 884744 | tf_op jit(solution)/shard_map/amplitudes/ppermute | solution.py:96
Sparse Core Ops, SparseCore 0:
  66.7 69.9 all-gather.1
where the time goes:
time: 265 us; the launch traced here: 264 us
  blocking collectives  76.8 us (29%)
  waiting for transfers between devices  75.8 us (29%)
  starting transfers between devices  71.6 us (27%)
  between operations  14.4 us (5%)
  local copies, waits for them, and re-layouts  14 us (5%)
  other arithmetic  5.86 us (2%)
  matrix products  5.51 us (2%)
    all_to_all x3, blocking collectives, exchange(): value = lax.all_to_all(value, axis, split_axis=0, concat_axis=0, tiled=True)  40.7 us
    all_to_all x4, starting transfers between devices, exchange(): value = lax.all_to_all(value, axis, split_axis=0, concat_axis=0, tiled=True)  32.4 us
    all_gather x1, waiting for transfers between devices, local(): lax.all_gather(row.reshape(nx * r, nocc * wide), 'z', axis=0, tiled=True)  25.6 us
    all_to_all x4, waiting for transfers between devices, exchange(): value = lax.all_to_all(value, axis, split_axis=0, concat_axis=0, tiled=True)  25.5 us
    ppermute x3, starting transfers between devices, swap_cores(): return lax.ppermute(value, 'c', [(0, 1), (1, 0)])  25 us
    ppermute x1, waiting for transfers between devices, local(): own = lax.ppermute(amps, ('z', 'c'), swap)  21.2 us
    ppermute x1, starting transfers between devices, local(): own = lax.ppermute(amps, ('z', 'c'), swap)  14.2 us
    all_gather x1, blocking collectives, local(): masked = lax.all_gather(masked.reshape(-1, ao_part), 'x', axis=0)  13.2 us
  transfers between devices with their start and end apart: 9, of which 8 were waited for; matrix products, arithmetic and copies ran while one was open for 2% of the time, Pallas kernels for 0%

commit v1 on v0

--- a/solution.py
+++ b/solution.py
@@ -6,6 +6,9 @@
 
 BF = jnp.bfloat16
 F32 = jnp.float32
+prepare_patches = lambda target, pos_dim: jnp.concatenate(
+    lax.all_to_all(jnp.stack([target for _ in range(lax.axis_size("z"))]), "z", 0, 0), axis=pos_dim
+)
 
 
 def swap_cores(value):
@@ -55,7 +58,7 @@
         three = jnp.sum(part.astype(F32), axis=0).astype(BF).reshape(nx, nocc, r, wide)
     with jax.named_scope("panels"):
         row = jnp.concatenate([three[:, i] for i in range(nocc)], axis=-1)
-        row = lax.all_gather(row.reshape(nx * r, nocc * wide), "z", axis=0, tiled=True)
+        row = prepare_patches(row.reshape(nx * r, nocc * wide), 0)
         col = exchange(three.reshape(nx, nocc * r, wide), "x")
         col = col.reshape(nx, nocc, r, ways // 2, 2, narrow)
         col = jnp.concatenate(

time: 265 us -> 356 us (1.34)
  waiting for transfers between devices: 75.8 us -> 173 us
  between operations: 14.4 us -> 1 us
  starting transfers between devices: 71.6 us -> 75.4 us
    all_to_all x0 -> x1, waiting for transfers between devices: none -> 125 us  [lax.all_to_all(jnp.stack([target for _ in range(lax.axis_size('z'))]), 'z...]
    all_gather x1 -> x0, waiting for transfers between devices: 25.6 us -> none  [local(): lax.all_gather(row.reshape(nx * r, nocc * wide), 'z', axis=0, tiled=True)]
    ppermute x3, starting transfers between devices: 25 us -> 18.1 us  [swap_cores(): return lax.ppermute(value, 'c', [(0, 1), (1, 0)])]
    all_to_all x0 -> x1, starting transfers between devices: none -> 6.08 us  [lax.all_to_all(jnp.stack([target for _ in range(lax.axis_size('z'))]), 'z...]
    all_to_all x4, starting transfers between devices: 32.4 us -> 37.6 us  [exchange(): value = lax.all_to_all(value, axis, split_axis=0, concat_axis=0, tiled=True)]
    all_to_all x4, waiting for transfers between devices: 25.5 us -> 21.6 us  [exchange(): value = lax.all_to_all(value, axis, split_axis=0, concat_axis=0, tiled=True)]
where the time goes in v1:
time: 356 us; the launch traced here: 355 us
  waiting for transfers between devices  173 us (49%)
  starting transfers between devices  75.4 us (21%)
  blocking collectives  73.5 us (21%)
  local copies, waits for them, and re-layouts  15.8 us (4%)
  other arithmetic  9.24 us (3%)
  matrix products  6.47 us (2%)
    all_to_all x1, waiting for transfers between devices, lax.all_to_all(jnp.stack([target for _ in range(lax.axis_size('z'))]), 'z...  125 us
    all_to_all x3, blocking collectives, exchange(): value = lax.all_to_all(value, axis, split_axis=0, concat_axis=0, tiled=True)  38.9 us
    all_to_all x4, starting transfers between devices, exchange(): value = lax.all_to_all(value, axis, split_axis=0, concat_axis=0, tiled=True)  37.6 us
    ppermute x1, waiting for transfers between devices, local(): own = lax.ppermute(amps, ('z', 'c'), swap)  22.9 us
    all_to_all x4, waiting for transfers between devices, exchange(): value = lax.all_to_all(value, axis, split_axis=0, concat_axis=0, tiled=True)  21.6 us
    ppermute x3, starting transfers between devices, swap_cores(): return lax.ppermute(value, 'c', [(0, 1), (1, 0)])  18.1 us
    ppermute x1, starting transfers between devices, local(): own = lax.ppermute(amps, ('z', 'c'), swap)  13.6 us
    all_gather x1, blocking collectives, local(): masked = lax.all_gather(masked.reshape(-1, ao_part), 'x', axis=0)  13.2 us
  transfers between devices with their start and end apart: 9, of which 8 were waited for; matrix products, arithmetic and copies ran while one was open for 2% of the time, Pallas kernels for 0%

profile of v1, /device:TPU:1, one launch (start us, length us, event | category | flops | bytes accessed | tf_op | source)
XLA Modules:
  0.0 354.6 jit_solution(8689925527877326871)
XLA Ops:
  0.6 1.5 broadcast_in_dim.10
  2.1 15.7 %all-to-all-start = ((bf16[16,16,640]{2,1,0:T(8,128)(2,1)}), bf16[16,16,640]{2,1,0:T(8,128)(2,1)S(1)}, u32[]{:S(2)}, u32[]{:S(2)}) async-start(bf16[16,16,640]{2,1,0:T(8,128)(2,1)} %broadcast_in_dim.10), calls=%async_computation | async-start | bytes 655360 | tf_op jit(solution)/shard_map/transform/all_to_all | solution.py:21
  17.9 0.7 convert_element_type.44
  18.7 1.0 broadcast_multiply_fusion
  19.7 13.2 %all_gather.9 = bf16[4,192,640]{2,1,0:T(8,128)(2,1)S(1)} all-gather(bf16[1,192,640]{2,1,0:T(8,128)(2,1)S(1)} %bitcast.116), channel_id=1, replica_groups=mesh['x'=4,'z'=16,'c'=2,'y'=4] {'x'}, dimensions={0}, use_global_device_ids=true | all-gather | bytes 1228800 | tf_op jit(solution)/shard_map/transform/all_gather | solution.py:51
  33.1 8.4 %collective-permute-start = (bf16[16,16,640]{2,1,0:T(8,128)(2,1)S(1)}, bf16[16,16,640]{2,1,0:T(8,128)(2,1)S(1)}, u32[]{:S(2)}, u32[]{:S(2)}) collective-permute-start(bf16[16,16,640]{2,1,0:T(8,128)(2,1)S(1)} %all-to-all-done), channel_id=1, source_target_pairs={{0,4},{4,0},{1,5},{5,1},{2,6},{6,2},{3,7},{7,3},{8,12},{12,8},{9,1... | collective-permute-start | bytes 983048 | tf_op jit(solution)/shard_map/transform/ppermute | solution.py:15
  41.5 1.2 collective-permute-done
  42.9 0.8 fusion
  43.8 15.4 %all_to_all.62 = bf16[4,192,512]{2,1,0:T(8,128)(2,1)S(1)} all-to-all(bf16[4,192,512]{2,1,0:T(8,128)(2,1)S(1)} %bitcast.105), channel_id=1, replica_groups=mesh['x'=4,'z'=16,'c'=2,'y'=4] {'y'}, dimensions={0} | all-to-all | bytes 1572864 | tf_op jit(solution)/shard_map/transform/all_to_all | solution.py:21
  59.3 9.0 %all_to_all.63 = bf16[4,48,512]{2,1,0:T(8,128)(2,1)S(1)} all-to-all(bf16[4,48,512]{2,1,0:T(8,128)(2,1)S(1)} %bitcast.112), channel_id=1, replica_groups=mesh['x'=4,'z'=16,'c'=2,'y'=4] {'x'}, dimensions={0} | all-to-all | bytes 393216 | tf_op jit(solution)/shard_map/panels/all_to_all | solution.py:21
  68.6 0.7 pad_maximum_fusion.2
  69.3 7.6 %all-to-all-start.4 = ((bf16[16,16,384]{2,1,0:T(8,128)(2,1)}), bf16[16,16,384]{2,1,0:T(8,128)(2,1)S(1)}, u32[]{:S(2)}, u32[]{:S(2)}) async-start(bf16[16,16,384]{2,1,0:T(8,128)(2,1)} %pad_maximum_fusion.2), calls=%async_computation.4 | async-start | bytes 393216 | tf_op jit(solution)/shard_map/panels/all_to_all | solution.py:21
  76.9 12.3 %all-to-all-done.4 = bf16[16,16,384]{2,1,0:T(8,128)(2,1)S(1)} async-done(((bf16[16,16,384]{2,1,0:T(8,128)(2,1)}), bf16[16,16,384]{2,1,0:T(8,128)(2,1)S(1)}, u32[]{:S(2)}, u32[]{:S(2)}) %all-to-all-start.4) | async-done | bytes 196640 | tf_op jit(solution)/shard_map/panels/all_to_all | solution.py:21
  89.2 1.9 stack.24
  91.1 6.1 %all-to-all-start.2 = ((bf16[16,64,1536]{2,1,0:T(8,128)(2,1)}), bf16[16,64,1536]{2,1,0:T(8,128)(2,1)S(1)}, u32[]{:S(2)}, u32[]{:S(2)}) async-start(bf16[16,64,1536]{2,1,0:T(8,128)(2,1)} %stack.24), calls=%async_computation.2 | async-start | bytes 6291456 | tf_op jit(solution)/shard_map/panels/all_to_all | solution.py:10
  97.2 11.0 %all_gather.10 = bf16[4,256,384]{2,1,0:T(8,128)(2,1)S(1)} all-gather(bf16[1,256,384]{2,1,0:T(8,128)(2,1)S(1)} %bitcast.121), channel_id=1, replica_groups=mesh['x'=4,'z'=16,'c'=2,'y'=4] {'x'}, dimensions={0}, use_global_device_ids=true | all-gather | bytes 983040 | tf_op jit(solution)/shard_map/panels/all_gather | solution.py:69
  108.2 1.0 copy.61
  109.2 124.8 %all-to-all-done.2 = bf16[16,64,1536]{2,1,0:T(8,128)(2,1)S(1)} async-done(((bf16[16,64,1536]{2,1,0:T(8,128)(2,1)}), bf16[16,64,1536]{2,1,0:T(8,128)(2,1)S(1)}, u32[]{:S(2)}, u32[]{:S(2)}) %all-to-all-start.2) | async-done | bytes 3145760 | tf_op jit(solution)/shard_map/panels/all_to_all | solution.py:10
  234.0 2.9 copy.57
  236.9 3.9 %fusion.5 = f32[3,2,256,384]{3,2,1,0:T(8,128)S(1)} fusion(bf16[3,2,256,1024]{3,2,1,0:T(8,128)(2,1)} %bitcast.104, bf16[1024,384,1,1]{1,0,3,2:T(8,128)(2,1)} %bitcast.119), kind=kOutput, calls=%fused_computation.31 | convolution fusion | flops 1207959552 | bytes 6291456 | tf_op jit(solution)/shard_map/gram/dot_general | solution.py:73
  240.8 1.4 copy-done
  242.2 1.1 dynamic-slice_bitcast_fusion
  243.3 3.4 collective-permute-start.1
  246.7 0.8 dynamic_slice.16
  247.5 0.8 dynamic_slice.15
  248.3 0.2 select_reduce_fusion
  248.4 1.0 collective-permute-done.1
  249.5 1.7 fusion.1
  251.2 0.9 copy.62
  252.1 4.1 %all-to-all-start.5 = ((bf16[4,192,384]{2,1,0:T(8,128)(2,1)}), bf16[4,192,384]{2,1,0:T(8,128)(2,1)}, u32[]{:S(2)}, u32[]{:S(2)}) async-start(bf16[4,192,384]{2,1,0:T(8,128)(2,1)} %bitcast.109), calls=%async_computation.5 | async-start | bytes 1179648 | tf_op jit(solution)/shard_map/gram/all_to_all | solution.py:21
  256.3 0.7 broadcast_subtract_fusion
  257.1 9.2 %all-to-all-done.5 = bf16[4,192,384]{2,1,0:T(8,128)(2,1)} async-done(((bf16[4,192,384]{2,1,0:T(8,128)(2,1)}), bf16[4,192,384]{2,1,0:T(8,128)(2,1)}, u32[]{:S(2)}, u32[]{:S(2)}) %all-to-all-start.5) | async-done | bytes 589856 | tf_op jit(solution)/shard_map/gram/all_to_all | solution.py:21
  266.3 1.2 convert_reduce_fusion
  267.4 0.9 reshape.202
  268.3 1.3 subtract_divide_fusion
  269.6 0.3 fusion.2
  270.0 10.4 %all_gather.11 = bf16[4,192,384]{2,1,0:T(8,128)(2,1)S(1)} all-gather(bf16[1,192,384]{2,1,0:T(8,128)(2,1)S(1)} %pad_maximum_fusion.3), channel_id=1, replica_groups=mesh['x'=4,'z'=16,'c'=2,'y'=4] {'y'}, dimensions={0}, use_global_device_ids=true | all-gather | bytes 737280 | tf_op jit(solution)/shard_map/amplitudes/all_gather | solution.py:101
  280.5 6.3 %collective-permute-start.3 = (bf16[3,256,384]{2,1,0:T(8,128)(2,1)S(1)}, bf16[3,256,384]{2,1,0:T(8,128)(2,1)S(1)}, u32[]{:S(2)}, u32[]{:S(2)}) collective-permute-start(bf16[3,256,384]{2,1,0:T(8,128)(2,1)S(1)} %bitcast.108), channel_id=1, source_target_pairs={{0,4},{4,0},{1,5},{5,1},{2,6},{6,2},{3,7},{7,3},{8,12},{12,8},{9,1... | collective-permute-start | bytes 1769480 | tf_op jit(solution)/shard_map/amplitudes/ppermute | solution.py:15
  286.8 1.6 collective-permute-done.3
  288.9 1.8 convolution_convert_fusion
  290.7 14.4 %all_to_all.64 = bf16[4,256,384]{2,1,0:T(8,128)(2,1)S(1)} all-to-all(bf16[4,256,384]{2,1,0:T(8,128)(2,1)S(1)} %bitcast.106), channel_id=1, replica_groups=mesh['x'=4,'z'=16,'c'=2,'y'=4] {'x'}, dimensions={0} | all-to-all | bytes 1572864 | tf_op jit(solution)/shard_map/gamma/all_to_all | solution.py:21
  305.2 0.8 reduce_sum.45
  306.0 10.2 %all-to-all-start.7 = ((bf16[16,16,384]{2,1,0:T(8,128)(2,1)}), bf16[16,16,384]{2,1,0:T(8,128)(2,1)S(1)}, u32[]{:S(2)}, u32[]{:S(2)}) async-start(bf16[16,16,384]{2,1,0:T(8,128)(2,1)} %bitcast.56), calls=%async_computation.7 | async-start | bytes 393216 | tf_op jit(solution)/shard_map/gamma/all_to_all | solution.py:21
  316.2 13.6 %collective-permute-start.2 = (f32[3,64,3,128]{3,2,1,0:T(4,128)S(1)}, f32[3,64,3,128]{3,2,1,0:T(4,128)S(1)}, u32[]{:S(2)}, u32[]{:S(2)}) collective-permute-start(f32[3,64,3,128]{3,2,1,0:T(4,128)S(1)} %subtract_divide_fusion), channel_id=1, source_target_pairs={{0,0},{4,64},{8,8},{12,72},{16,16},{20,80},{24,24},{28,88},{32,32}... | collective-permute-start | bytes 884744 | tf_op jit(solution)/shard_map/amplitudes/ppermute | solution.py:99
  329.8 22.9 %collective-permute-done.2 = f32[3,64,3,128]{3,2,1,0:T(4,128)S(1)} collective-permute-done((f32[3,64,3,128]{3,2,1,0:T(4,128)S(1)}, f32[3,64,3,128]{3,2,1,0:T(4,128)S(1)}, u32[]{:S(2)}, u32[]{:S(2)}) %collective-permute-start.2) | collective-permute-done | bytes 294944 | tf_op jit(solution)/shard_map/amplitudes/ppermute | solution.py:99
  352.7 0.7 copy.71
  353.5 0.2 copy.70
  353.8 0.8 reshape.208
  (34 shorter events, 1.8 us)
Async XLA Ops:
  2.1 31.0 %all-to-all-start = ((bf16[16,16,640]{2,1,0:T(8,128)(2,1)}), bf16[16,16,640]{2,1,0:T(8,128)(2,1)S(1)}, u32[]{:S(2)}, u32[]{:S(2)}) async-start(bf16[16,16,640]{2,1,0:T(8,128)(2,1)} %broadcast_in_dim.10), calls=%async_computation | async-start | bytes 655360 | tf_op jit(solution)/shard_map/transform/all_to_all | solution.py:21
  33.1 9.6 %collective-permute-start = (bf16[16,16,640]{2,1,0:T(8,128)(2,1)S(1)}, bf16[16,16,640]{2,1,0:T(8,128)(2,1)S(1)}, u32[]{:S(2)}, u32[]{:S(2)}) collective-permute-start(bf16[16,16,640]{2,1,0:T(8,128)(2,1)S(1)} %all-to-all-done), channel_id=1, source_target_pairs={{0,4},{4,0},{1,5},{5,1},{2,6},{6,2},{3,7},{7,3},{8,12},{12,8},{9,1... | collective-permute-start | bytes 983048 | tf_op jit(solution)/shard_map/transform/ppermute | solution.py:15
  69.3 19.9 %all-to-all-start.4 = ((bf16[16,16,384]{2,1,0:T(8,128)(2,1)}), bf16[16,16,384]{2,1,0:T(8,128)(2,1)S(1)}, u32[]{:S(2)}, u32[]{:S(2)}) async-start(bf16[16,16,384]{2,1,0:T(8,128)(2,1)} %pad_maximum_fusion.2), calls=%async_computation.4 | async-start | bytes 393216 | tf_op jit(solution)/shard_map/panels/all_to_all | solution.py:21
  91.1 142.9 %all-to-all-start.2 = ((bf16[16,64,1536]{2,1,0:T(8,128)(2,1)}), bf16[16,64,1536]{2,1,0:T(8,128)(2,1)S(1)}, u32[]{:S(2)}, u32[]{:S(2)}) async-start(bf16[16,64,1536]{2,1,0:T(8,128)(2,1)} %stack.24), calls=%async_computation.2 | async-start | bytes 6291456 | tf_op jit(solution)/shard_map/panels/all_to_all | solution.py:10
  240.8 1.4 copy-start
  242.2 6.0 %copy-start.1 = (f32[512]{0:T(512)S(1)}, f32[512]{0:T(512)}, u32[]{:S(2)}) copy-start(f32[512]{0:T(512)} %param.9) | copy-start | bytes 6148
  242.2 6.0 %copy-start.2 = (s32[3]{0:T(128)S(1)}, s32[3]{0:T(128)}, u32[]{:S(2)}) copy-start(s32[3]{0:T(128)} %param.11) | copy-start | bytes 40
  243.3 6.2 %collective-permute-start.1 = (f32[3,256,384]{2,1,0:T(8,128)}, f32[3,256,384]{2,1,0:T(8,128)}, u32[]{:S(2)}, u32[]{:S(2)}) collective-permute-start(f32[3,256,384]{2,1,0:T(8,128)} %dynamic-slice_bitcast_fusion), channel_id=1, source_target_pairs={{0,4},{4,0},{1,5},{5,1},{2,6},{6,2},{3,7},{7,3},{8,12},{12,8},{9,1... | collective-permute-start | bytes 3538952 | tf_op jit(solution)/shard_map/gram/ppermute | solution.py:15
  252.1 14.1 %all-to-all-start.5 = ((bf16[4,192,384]{2,1,0:T(8,128)(2,1)}), bf16[4,192,384]{2,1,0:T(8,128)(2,1)}, u32[]{:S(2)}, u32[]{:S(2)}) async-start(bf16[4,192,384]{2,1,0:T(8,128)(2,1)} %bitcast.109), calls=%async_computation.5 | async-start | bytes 1179648 | tf_op jit(solution)/shard_map/gram/all_to_all | solution.py:21
  280.5 7.9 %collective-permute-start.3 = (bf16[3,256,384]{2,1,0:T(8,128)(2,1)S(1)}, bf16[3,256,384]{2,1,0:T(8,128)(2,1)S(1)}, u32[]{:S(2)}, u32[]{:S(2)}) collective-permute-start(bf16[3,256,384]{2,1,0:T(8,128)(2,1)S(1)} %bitcast.108), channel_id=1, source_target_pairs={{0,4},{4,0},{1,5},{5,1},{2,6},{6,2},{3,7},{7,3},{8,12},{12,8},{9,1... | collective-permute-start | bytes 1769480 | tf_op jit(solution)/shard_map/amplitudes/ppermute | solution.py:15
  306.0 47.4 %all-to-all-start.7 = ((bf16[16,16,384]{2,1,0:T(8,128)(2,1)}), bf16[16,16,384]{2,1,0:T(8,128)(2,1)S(1)}, u32[]{:S(2)}, u32[]{:S(2)}) async-start(bf16[16,16,384]{2,1,0:T(8,128)(2,1)} %bitcast.56), calls=%async_computation.7 | async-start | bytes 393216 | tf_op jit(solution)/shard_map/gamma/all_to_all | solution.py:21
  316.2 36.5 %collective-permute-start.2 = (f32[3,64,3,128]{3,2,1,0:T(4,128)S(1)}, f32[3,64,3,128]{3,2,1,0:T(4,128)S(1)}, u32[]{:S(2)}, u32[]{:S(2)}) collective-permute-start(f32[3,64,3,128]{3,2,1,0:T(4,128)S(1)} %subtract_divide_fusion), channel_id=1, source_target_pairs={{0,0},{4,64},{8,8},{12,72},{16,16},{20,80},{24,24},{28,88},{32,32}... | collective-permute-start | bytes 884744 | tf_op jit(solution)/shard_map/amplitudes/ppermute | solution.py:99
